TPU v7x, 256 devices: a whole 4x4x8 slice. The times are simulated.
256 devices in a mesh: out: 128 (over z, y, x), con: 2 (over core).
Axes of the slice: x: 4, y: 4, z: 8, core: 2. Of those that a mesh axis runs over, the one named last changes fastest.
Arguments:
- amplitudes: bfloat16 [512, 9216], P(('out', 'con')), may hold values from -6 to 6
- integrals: bfloat16 [131072, 9216], P('out', 'con'), may hold values from -0.078125 to 0.078125
- block_sizes: int32 [8], replicated, may hold values from 64 to 192, as said below
Outputs:
- ladder: bfloat16 [512, 131072], P('con', 'out')
Inputs may be any that keep to these rules, and one draw needn't show every extreme that they name: `block_sizes`: each entry lies between 64 and 192; the entries sum to 1024; one entry equals 192 and one equals 64.
All inputs are finite; a program needn't handle non-finite values.
Results may differ from a plain program's by a relative error of at most 0.001.
Values may be sent and summed in bfloat16 or wider, within the bound.
A program may use at most 64 MiB of HBM per device.

v0:
```python
import jax
import jax.numpy as jnp
from jax import lax
from jax.sharding import Mesh, PartitionSpec as P

DMAX = 192
TORUS = {128: (("z", 8), ("y", 4), ("x", 4))}


def mask_slots(amplitudes, block_sizes):
    row_count = amplitudes.shape[0]
    nirrep = block_sizes.shape[0]
    blocked = amplitudes.reshape(row_count, nirrep, -1, DMAX)
    valid_cols = jnp.arange(DMAX, dtype=jnp.int32)[None, :] < block_sizes[:, None]
    masked = jnp.where(valid_cols[None, :, None, :], blocked, jnp.zeros((), amplitudes.dtype))
    return masked.reshape(row_count, -1)


def contract(amp_rows, integrals):
    return lax.dot_general(
        amp_rows, integrals, (((1,), (1,)), ((), ())), preferred_element_type=jnp.float32
    )


def make_on_device(out_axes):

    def on_device(amplitudes, integrals, block_sizes):
        masked = mask_slots(amplitudes, block_sizes)
        con = lax.axis_index("con")
        con_count = lax.axis_size("con")
        half = integrals.shape[1]
        chip_rows = lax.all_gather(masked, "con", axis=0, tiled=True)
        all_rows = lax.dynamic_slice_in_dim(chip_rows, con * half, half, axis=1)
        for name in reversed(out_axes):
            all_rows = lax.all_gather(all_rows, name, axis=0, tiled=True)
        out_rows = all_rows.shape[0] // con_count
        other = 1 - con
        other_part = contract(
            lax.dynamic_slice_in_dim(all_rows, other * out_rows, out_rows, axis=0), integrals
        )
        received = lax.ppermute(other_part, "con", perm=[(0, 1), (1, 0)])
        own_part = contract(
            lax.dynamic_slice_in_dim(all_rows, con * out_rows, out_rows, axis=0), integrals
        )
        own_part = lax.optimization_barrier(own_part)
        return (own_part + received).astype(jnp.bfloat16)

    return on_device


def solution(mesh):
    n_out = mesh.shape["out"]
    axes = TORUS.get(n_out, (("out", n_out),))
    names = tuple((name for name, _ in axes))
    devices = mesh.devices.reshape(tuple((size for _, size in axes)) + (mesh.shape["con"],))
    torus_mesh = Mesh(devices, names + ("con",))
    in_specs = (P(names + ("con",), None), P(names, "con"), P())
    out_specs = P("con", names)
    return jax.shard_map(
        make_on_device(names),
        mesh=torus_mesh,
        in_specs=in_specs,
        out_specs=out_specs,
        check_vma=False,
    )
```

profile of v0, /device:TPU:1, one launch (start us, length us, event | category | flops | bytes accessed | tf_op | source)
XLA Modules:
  0.0 119.7 jit_solution(11476787945079464817)
XLA Ops:
  6.5 0.0 all-gather.4.cloned.1.call-start
  6.5 0.7 iota_compare_fusion
  7.3 0.1 broadcast_in_dim.20
  7.4 0.8 fusion.4
  8.2 4.8 %all-gather = bf16[2,2,9216]{2,1,0:T(2,128)(2,1)S(1)} all-gather(bf16[1,2,9216]{2,1,0:T(2,128)(2,1)S(1)} %fusion.4), channel_id=1, replica_groups=mesh['z'=8,'y'=4,'x'=4,'con'=2] {'con'}, dimensions={0}, use_global_device_ids=true | all-gather | bytes 110592 | tf_op jit(solution)/shard_map/all_gather | solution.py:32
  13.0 9.1 %all-gather.1 = bf16[4,4,4608]{2,1,0:T(4,128)(2,1)S(1)} all-gather(bf16[1,4,4608]{2,1,0:T(4,128)(2,1)S(1)} %dynamic-slice_bitcast_fusion), channel_id=1, replica_groups=mesh['z'=8,'y'=4,'x'=4,'con'=2] {'x'}, dimensions={0}, use_global_device_ids=true | all-gather | bytes 184320 | tf_op jit(solution)/shard_map/all_gather | solution.py:35
  22.2 10.8 %all_gather.14 = bf16[64,4608]{1,0:T(8,128)(2,1)} all-gather(bf16[16,4608]{1,0:T(8,128)(2,1)S(1)} %reshape.24), channel_id=1, replica_groups=mesh['z'=8,'y'=4,'x'=4,'con'=2] {'y'}, dimensions={0}, use_global_device_ids=true | all-gather | bytes 737280 | tf_op jit(solution)/shard_map/all_gather | solution.py:35
  33.0 0.0 all-gather.4.cloned.1.call-update
  33.0 66.2 %all-gather.4.cloned.1.call-done = bf16[512,4608]{1,0:T(8,128)(2,1)} async-done(((bf16[64,4608]{1,0:T(8,128)(2,1)}), bf16[512,4608]{1,0:T(8,128)(2,1)}) %all-gather.4.cloned.1.call-update) | async-done | bytes 4718608 | tf_op jit(solution)/shard_map/all_gather | solution.py:35
  99.2 6.0 %fusion = f32[256,1024]{1,0:T(8,128)S(1)} fusion(bf16[1024,4608]{1,0:T(8,128)(2,1)} %param.4, bf16[512,4608]{1,0:T(8,128)(2,1)} %all-gather.4.cloned.1.call-done, s32[]{:T(128)S(6)} %select_n.17), kind=kOutput, calls=%fused_computation | convolution fusion | flops 2415919104 | bytes 12845060 | tf_op jit(solution)/shard_map/dot_general | solution.py:20
  105.2 0.8 collective-permute-start
  105.9 6.0 %fusion.2 = f32[256,1024]{1,0:T(8,128)S(1)} fusion(bf16[1024,4608]{1,0:T(8,128)(2,1)} %param.4, bf16[512,4608]{1,0:T(8,128)(2,1)} %all-gather.4.cloned.1.call-done, s32[]{:T(128)S(6)} %select_n.16), kind=kOutput, calls=%fused_computation.2 | convolution fusion | flops 2415919104 | bytes 12845060 | tf_op jit(solution)/shard_map/dot_general | solution.py:20
  111.9 0.0 collective-permute-done
  111.9 1.0 add_convert_fusion
  (4 shorter events, 0.1 us)
Async XLA Ops:
  6.5 92.7 %all-gather.4.cloned.1.call-start = ((), (), s32[]{:S(2)}) async-start(), calls=%async_computation | async-start | bytes 5308416 | tf_op jit(solution)/shard_map/all_gather | solution.py:35
  105.2 6.7 %collective-permute-start = (f32[256,1024]{1,0:T(8,128)S(1)}, f32[256,1024]{1,0:T(8,128)S(1)}, u32[]{:S(2)}, u32[]{:S(2)}) collective-permute-start(f32[256,1024]{1,0:T(8,128)S(1)} %fusion), channel_id=1, source_target_pairs={{0,1},{1,0},{2,3},{3,2},{4,5},{5,4},{6,7},{7,6},{8,9},{9,8},{10,11... | collective-permute-start | bytes 3145736 | tf_op jit(solution)/shard_map/ppermute | solution.py:41
Sparse Core Ops, SparseCore 0:
  33.1 66.0 all-gather.3
where the time goes:
time: 120 us
  waiting for transfers between devices  66.2 us (55%)
  blocking collectives  24.7 us (21%)
  between operations  13.4 us (11%)
  matrix products  11.9 us (10%)
  other arithmetic  2.51 us (2%)
    all_gather x1, waiting for transfers between devices, on_device(): all_rows = lax.all_gather(all_rows, name, axis=0, tiled=True)  66.2 us
    all_gather x2, blocking collectives, on_device(): all_rows = lax.all_gather(all_rows, name, axis=0, tiled=True)  19.9 us
    dot_general x2, matrix products, contract(): lax.dot_general(amp_rows, integrals, (((1,), (1,)), ((), ())), preferred_...  11.9 us
    all_gather x1, blocking collectives, on_device(): chip_rows = lax.all_gather(masked, 'con', axis=0, tiled=True)  4.75 us
  transfers between devices with their start and end apart: 2, of which 1 were waited for; matrix products, arithmetic and copies ran while one was open for 5% of the time, Pallas kernels for 0%

commit v1 on v0

--- a/solution.py
+++ b/solution.py
@@ -5,6 +5,13 @@
 
 DMAX = 192
 TORUS = {128: (("z", 8), ("y", 4), ("x", 4))}
+
+
+def swapped_in(value, axis, along):
+    n_dev = lax.axis_size(axis)
+    blocks = jnp.stack([value for _ in range(n_dev)])
+    blocks = lax.all_to_all(blocks, axis, split_axis=0, concat_axis=0)
+    return jnp.concatenate(blocks, axis=along)
 
 
 def mask_slots(amplitudes, block_sizes):
@@ -32,7 +39,7 @@
         chip_rows = lax.all_gather(masked, "con", axis=0, tiled=True)
         all_rows = lax.dynamic_slice_in_dim(chip_rows, con * half, half, axis=1)
         for name in reversed(out_axes):
-            all_rows = lax.all_gather(all_rows, name, axis=0, tiled=True)
+            all_rows = swapped_in(all_rows, name, 0)
         out_rows = all_rows.shape[0] // con_count
         other = 1 - con
         other_part = contract(

time: 120 us -> 158 us (1.32)
  waiting for transfers between devices: 66.2 us -> 104 us
  between operations: 13.4 us -> 0.06 us
  starting transfers between devices: 0.76 us -> 12.7 us
  local copies, waits for them, and re-layouts: 0.22 us -> 2.85 us
    all_to_all x0 -> x1, waiting for transfers between devices: none -> 104 us  [swapped_in(): blocks = lax.all_to_all(blocks, axis, split_axis=0, concat_axis=0)]
    all_gather x1 -> x0, waiting for transfers between devices: 66.2 us -> none  [on_device(): all_rows = lax.all_gather(all_rows, name, axis=0, tiled=True)]
    all_gather x2 -> x0, blocking collectives: 19.9 us -> none  [on_device(): all_rows = lax.all_gather(all_rows, name, axis=0, tiled=True)]
    all_to_all x0 -> x2, blocking collectives: none -> 19.1 us  [swapped_in(): blocks = lax.all_to_all(blocks, axis, split_axis=0, concat_axis=0)]
    all_to_all x0 -> x1, starting transfers between devices: none -> 8.19 us  [swapped_in(): blocks = lax.all_to_all(blocks, axis, split_axis=0, concat_axis=0)]
    ppermute x1, starting transfers between devices: 0.76 us -> 4.54 us  [on_device(): received = lax.ppermute(other_part, 'con', perm=[(0, 1), (1, 0)])]
    another operation x0 -> x4, local copies, waits for them, and re-layouts: none -> 2.67 us  [swapped_in(): blocks = jnp.stack([value for _ in range(n_dev)])]
  transfers between devices with their start and end apart: 2 -> 2, of which waited for: 1 -> 1; matrix products, arithmetic and copies ran while one was open for 5% -> 4% of each run, Pallas kernels for 0% -> 0%
where the time goes in v1:
time: 158 us
  waiting for transfers between devices  104 us (66%)
  blocking collectives  23.9 us (15%)
  starting transfers between devices  12.7 us (8%)
  matrix products  11.9 us (8%)
  local copies, waits for them, and re-layouts  2.85 us (2%)
  other arithmetic  2.51 us (2%)
    all_to_all x1, waiting for transfers between devices, swapped_in(): blocks = lax.all_to_all(blocks, axis, split_axis=0, concat_axis=0)  104 us
    all_to_all x2, blocking collectives, swapped_in(): blocks = lax.all_to_all(blocks, axis, split_axis=0, concat_axis=0)  19.1 us
    dot_general x2, matrix products, contract(): lax.dot_general(amp_rows, integrals, (((1,), (1,)), ((), ())), preferred_...  11.9 us
    all_to_all x1, starting transfers between devices, swapped_in(): blocks = lax.all_to_all(blocks, axis, split_axis=0, concat_axis=0)  8.19 us
    all_gather x1, blocking collectives, on_device(): chip_rows = lax.all_gather(masked, 'con', axis=0, tiled=True)  4.75 us
    ppermute x1, starting transfers between devices, on_device(): received = lax.ppermute(other_part, 'con', perm=[(0, 1), (1, 0)])  4.54 us
  transfers between devices with their start and end apart: 2, of which 1 were waited for; matrix products, arithmetic and copies ran while one was open for 4% of the time, Pallas kernels for 0%

profile of v1, /device:TPU:1, one launch (start us, length us, event | category | flops | bytes accessed | tf_op | source)
XLA Modules:
  0.0 158.1 jit_solution(13865362904883242295)
XLA Ops:
  0.0 0.7 iota_compare_fusion
  0.7 0.1 broadcast_in_dim.20
  0.9 0.8 fusion.4
  1.7 4.8 %all-gather = bf16[2,2,9216]{2,1,0:T(2,128)(2,1)S(1)} all-gather(bf16[1,2,9216]{2,1,0:T(2,128)(2,1)S(1)} %fusion.4), channel_id=1, replica_groups=mesh['z'=8,'y'=4,'x'=4,'con'=2] {'con'}, dimensions={0}, use_global_device_ids=true | all-gather | bytes 110592 | tf_op jit(solution)/shard_map/all_gather | solution.py:39
  6.6 7.3 %all_to_all.15 = bf16[4,4,4608]{2,1,0:T(4,128)(2,1)S(1)} all-to-all(bf16[4,4,4608]{2,1,0:T(4,128)(2,1)S(1)} %stack.6), channel_id=1, replica_groups=mesh['z'=8,'y'=4,'x'=4,'con'=2] {'x'}, dimensions={0} | all-to-all | bytes 294912 | tf_op jit(solution)/shard_map/all_to_all | solution.py:13
  13.9 11.9 %all_to_all.16 = bf16[4,16,4608]{2,1,0:T(8,128)(2,1)S(1)} all-to-all(bf16[4,16,4608]{2,1,0:T(8,128)(2,1)S(1)} %stack.14), channel_id=1, replica_groups=mesh['z'=8,'y'=4,'x'=4,'con'=2] {'y'}, dimensions={0} | all-to-all | bytes 1179648 | tf_op jit(solution)/shard_map/all_to_all | solution.py:13
  25.8 2.6 %stack.15 = bf16[8,64,4608]{2,1,0:T(8,128)(2,1)} broadcast(bf16[64,4608]{1,0:T(8,128)(2,1)S(1)} %bitcast.6), dimensions={1,2} | broadcast | bytes 5308416 | tf_op jit(solution)/shard_map/stack | solution.py:12
  28.3 8.2 %all-to-all-start.2 = ((bf16[8,64,4608]{2,1,0:T(8,128)(2,1)}), bf16[8,64,4608]{2,1,0:T(8,128)(2,1)}, u32[]{:S(2)}, u32[]{:S(2)}) async-start(bf16[8,64,4608]{2,1,0:T(8,128)(2,1)} %stack.15), calls=%async_computation.2 | async-start | bytes 9437184 | tf_op jit(solution)/shard_map/all_to_all | solution.py:13
  36.5 104.1 %all-to-all-done.2 = bf16[8,64,4608]{2,1,0:T(8,128)(2,1)} async-done(((bf16[8,64,4608]{2,1,0:T(8,128)(2,1)}), bf16[8,64,4608]{2,1,0:T(8,128)(2,1)}, u32[]{:S(2)}, u32[]{:S(2)}) %all-to-all-start.2) | async-done | bytes 4718624 | tf_op jit(solution)/shard_map/all_to_all | solution.py:13
  140.6 6.0 %fusion = f32[256,1024]{1,0:T(8,128)S(1)} fusion(bf16[1024,4608]{1,0:T(8,128)(2,1)} %param.4, bf16[512,4608]{1,0:T(8,128)(2,1)} %bitcast.2, s32[]{:T(128)S(6)} %select_n.17), kind=kOutput, calls=%fused_computation | convolution fusion | flops 2415919104 | bytes 12845060 | tf_op jit(solution)/shard_map/dot_general | solution.py:27
  146.6 4.5 %collective-permute-start = (f32[256,1024]{1,0:T(8,128)S(1)}, f32[256,1024]{1,0:T(8,128)S(1)}, u32[]{:S(2)}, u32[]{:S(2)}) collective-permute-start(f32[256,1024]{1,0:T(8,128)S(1)} %fusion), channel_id=1, source_target_pairs={{0,1},{1,0},{2,3},{3,2},{4,5},{5,4},{6,7},{7,6},{8,9},{9,8},{10,11... | collective-permute-start | bytes 3145736 | tf_op jit(solution)/shard_map/ppermute | solution.py:48
  151.2 6.0 %fusion.2 = f32[256,1024]{1,0:T(8,128)S(1)} fusion(bf16[1024,4608]{1,0:T(8,128)(2,1)} %param.4, bf16[512,4608]{1,0:T(8,128)(2,1)} %bitcast.2, s32[]{:T(128)S(6)} %select_n.16), kind=kOutput, calls=%fused_computation.2 | convolution fusion | flops 2415919104 | bytes 12845060 | tf_op jit(solution)/shard_map/dot_general | solution.py:27
  157.1 0.0 collective-permute-done
  157.1 1.0 add_convert_fusion
  (6 shorter events, 0.2 us)
Async XLA Ops:
  28.3 112.3 %all-to-all-start.2 = ((bf16[8,64,4608]{2,1,0:T(8,128)(2,1)}), bf16[8,64,4608]{2,1,0:T(8,128)(2,1)}, u32[]{:S(2)}, u32[]{:S(2)}) async-start(bf16[8,64,4608]{2,1,0:T(8,128)(2,1)} %stack.15), calls=%async_computation.2 | async-start | bytes 9437184 | tf_op jit(solution)/shard_map/all_to_all | solution.py:13
  146.6 10.5 %collective-permute-start = (f32[256,1024]{1,0:T(8,128)S(1)}, f32[256,1024]{1,0:T(8,128)S(1)}, u32[]{:S(2)}, u32[]{:S(2)}) collective-permute-start(f32[256,1024]{1,0:T(8,128)S(1)} %fusion), channel_id=1, source_target_pairs={{0,1},{1,0},{2,3},{3,2},{4,5},{5,4},{6,7},{7,6},{8,9},{9,8},{10,11... | collective-permute-start | bytes 3145736 | tf_op jit(solution)/shard_map/ppermute | solution.py:48
